TPU v7x, 32 devices: a whole 2x2x4 slice. The times are simulated.
32 devices in a mesh: frames: 8 (over y, x, core), planes: 4 (over z).
Axes of the slice: x: 2, y: 2, z: 4, core: 2. Of those that a mesh axis runs over, the one named last changes fastest.
Arguments:
- recording: float32 [64, 4, 256, 128], P('frames', 'planes'), may hold values from -30 to 30
- template: float32 [4, 256, 128], P('planes'), may hold values from -4 to 4
- shifts: int32 [64, 4, 2], P('frames', 'planes'), may hold values from -16 to 16
- support: int32 [256, 48], replicated, may hold values from 0 to 127, as said below
- temporal_init: float32 [64, 256], replicated, may hold values from 0 to 0.3
- spatial_init: float32 [256, 4, 32768], P(None, 'planes', 'frames'), may hold values from 0 to 29
Outputs:
- temporal: float32 [64, 256], replicated
- spatial: float32 [256, 4, 32768], P(None, 'planes', 'frames')
Inputs may be any that keep to these rules, and one draw needn't show every extreme that they name: `support`: each component names 48 different tiles.
All inputs are finite; a program needn't handle non-finite values.
Results may differ from a plain program's by a relative error of at most 0.0001.
Values sent between devices are 32-bit elements; how exact they have to be, the bound alone decides.
A program may use at most 128 MiB of HBM per device.

v0:
```python
import jax
import jax.numpy as jnp
from jax import lax
from jax.sharding import PartitionSpec as P

HEIGHT = 256
WIDTH = 128
TILE = 1024
NTREND = 16


epsilon = 1e-06


def matmul(left_side, right_side):
    return jnp.dot(
        left_side, right_side, precision=lax.Precision.HIGHEST, preferred_element_type=jnp.float32
    )


def cosine_table(frame_count, basis_order):
    times = jnp.arange(frame_count).astype(jnp.float32)
    orders = jnp.arange(basis_order).astype(jnp.float32)
    scales = jnp.where(
        orders == 0, jnp.sqrt(1.0 / frame_count), jnp.sqrt(2.0 / frame_count)
    ).astype(jnp.float32)
    return (
        jnp.cos(jnp.pi * (times[:, None] + 0.5) * orders[None, :] / frame_count) * scales[None, :]
    )


def shift_frame(picture, offsets):
    return jnp.roll(picture, (offsets[0], offsets[1]), axis=(0, 1))


def body(recording, template, shifts, support, temporal_init, spatial_init):
    frame_local = recording.shape[0]
    plane_local = recording.shape[1]
    pixel_count = HEIGHT * WIDTH
    registered = jax.vmap(jax.vmap(shift_frame))(recording, shifts)
    numerator = jnp.sum(registered * template[None], axis=(1, 2, 3))
    energy = jnp.sum(registered * registered, axis=(1, 2, 3))
    template_energy = jnp.sum(template * template)
    flattened = registered.reshape(frame_local, plane_local, pixel_count)
    numerator, energy, template_energy = lax.psum((numerator, energy, template_energy), "planes")
    weight = numerator / jnp.sqrt(energy * template_energy + epsilon)
    payload = flattened * weight[:, None, None]
    series = lax.all_to_all(payload, "frames", split_axis=2, concat_axis=0, tiled=True)
    frames_total = series.shape[0]
    pixels_local = series.shape[2]
    series = series.reshape(frames_total, plane_local * pixels_local)
    cosine_basis = cosine_table(frames_total, NTREND)
    detrended = series - matmul(cosine_basis, matmul(cosine_basis.T, series))
    frame_index = lax.axis_index("frames")
    plane_index = lax.axis_index("planes")
    local_tiles = pixels_local // TILE
    tile_ids = (
        plane_index * (pixel_count // TILE)
        + frame_index * pixels_local // TILE
        + jnp.arange(local_tiles)
    )
    covered = jnp.any(support[:, :, None] == tile_ids[None, None, :], axis=1).astype(jnp.float32)
    components = covered.shape[0]
    support_mask = jnp.broadcast_to(covered[:, :, None], (components, local_tiles, TILE)).reshape(
        components, local_tiles * TILE
    )
    spatial = spatial_init.reshape(components, plane_local * pixels_local) * support_mask
    temporal = temporal_init
    spatial_gram, cross = lax.psum(
        (matmul(spatial, spatial.T), matmul(detrended, spatial.T)), ("frames", "planes")
    )
    temporal_grad = matmul(temporal, spatial_gram) - cross
    grad_square = jnp.sum(temporal_grad * temporal_grad)
    grad_curve = jnp.sum(temporal_grad * matmul(temporal_grad, spatial_gram))
    temporal = jnp.maximum(temporal - grad_square / (grad_curve + epsilon) * temporal_grad, 0.0)
    temporal_gram = matmul(temporal.T, temporal)
    spatial_grad = (matmul(temporal_gram, spatial) - matmul(temporal.T, detrended)) * support_mask
    grad_square, grad_curve = lax.psum(
        (
            jnp.sum(spatial_grad * spatial_grad),
            jnp.sum(spatial_grad * matmul(temporal_gram, spatial_grad)),
        ),
        ("frames", "planes"),
    )
    spatial = jnp.maximum(spatial - grad_square / (grad_curve + epsilon) * spatial_grad, 0.0)
    return (temporal, spatial.reshape(components, plane_local, pixels_local))


def solution(mesh):
    placed = (
        P("frames", "planes", None, None),
        P("planes", None, None),
        P("frames", "planes", None),
        P(),
        P(),
        P(None, "planes", "frames"),
    )
    return jax.shard_map(
        body,
        mesh=mesh,
        in_specs=placed,
        out_specs=(P(), P(None, "planes", "frames")),
        check_vma=False,
    )
```

profile of v0, /device:TPU:0, one launch (start us, length us, event | category | flops | bytes accessed | tf_op | source)
XLA Modules:
  0.0 558.9 jit_solution(5631216840889842316)
XLA Ops:
  7.2 0.8 compare_select_fusion
  7.9 2.3 copy.33
  10.2 1.8 pad_maximum_fusion
  12.1 2.1 gather_fusion
  14.2 1.5 pad_maximum_fusion.1
  15.6 3.8 copy.35
  19.4 0.6 multiply_reduce_fusion.1
  20.1 0.1 copy.37
  20.2 1.7 gather_fusion.1
  21.9 0.4 copy.36
  22.3 0.4 fusion.9
  22.7 0.2 reshape.126
  22.9 14.3 %all-reduce.4 = (f32[8]{0:T(128)S(1)}, f32[8]{0:T(128)S(1)}, f32[]{:T(128)}) all-reduce(f32[8]{0:T(128)S(1)} %get-tuple-element.11, f32[8]{0:T(128)S(1)} %get-tuple-element.10, f32[]{:T(128)} %multiply_reduce_fusion.1), channel_id=1, replica_groups=mesh['frames'=8,'planes'=4] {'planes'}, use_global_device_ids=true, to_apply=%region_3.4 | all-reduce | flops 17 | bytes 136 | tf_op jit(solution)/shard_map/psum | solution.py:45
  37.3 0.7 rsqrt_multiply_fusion
  37.9 0.1 broadcast_multiply_fusion
  38.1 23.8 %copy.38 = f32[8,1,32768]{0,1,2:T(1,128)} copy(f32[8,1,32768]{2,0,1:T(8,128)S(1)} %broadcast_multiply_fusion) | data formatting | bytes 2097152 | tf_op jit(solution)/shard_map/mul | solution.py:47
  61.8 0.5 broadcast.199
  62.3 146.5 %reduce = f32[32768,8]{1,0:T(8,128)} reduce(f32[32768,1,8]{2,1,0:T(1,128)} %bitcast.60, f32[]{:T(128)} %broadcast.199), dimensions={1}, to_apply=%bitcast.40.reduce_sub_computation | reduce | bytes 2097156
  208.9 13.0 %reshape.148 = f32[8,1,32768]{2,1,0:T(1,128)} reshape(f32[32768,8]{1,0:T(8,128)} %reduce) | data formatting | bytes 2097152
  221.9 3.7 all-to-all-start
  225.6 0.0 all-reduce.7.cloned.1.call-start
  225.7 0.1 compare_reduce_fusion
  225.8 0.1 copy.32
  225.9 2.6 broadcast_in_dim.14
  228.5 8.6 %reshape.125 = f32[256,1,4096]{2,1,0:T(1,128)} reshape(f32[256,4,1024]{2,1,0:T(4,128)} %broadcast_in_dim.14) | data formatting | bytes 8388608 | tf_op jit(solution)/shard_map/reshape | solution.py:64
  237.1 7.9 %copy.45 = f32[32,8,4,1024]{3,1,2,0:T(8,128)} copy(f32[32,8,4,1024]{3,2,1,0:T(4,128)} %bitcast.62) | data formatting | bytes 8388608
  245.0 13.6 %mul.142 = f32[256,1,4096]{2,1,0:T(1,128)} multiply(f32[256,1,4096]{2,1,0:T(1,128)} %param.11, f32[256,1,4096]{2,1,0:T(1,128)} %reshape.125) | non-fusion elementwise | flops 1048576 | bytes 12582912 | tf_op jit(solution)/shard_map/mul | solution.py:67
  258.6 12.1 %fusion.1 = f32[256,256]{1,0:T(8,128)} fusion(f32[256,1,4096]{2,1,0:T(1,128)} %mul.142), kind=kOutput, calls=%fused_computation.7 | convolution fusion | flops 3221225472 | bytes 4456448 | tf_op jit(solution)/shard_map/dot_general | solution.py:16
  270.8 3.1 reduce.1
  273.9 39.7 %reshape.149 = f32[32768,1,8]{2,1,0:T(1,128)} reshape(f32[8,32768]{1,0:T(8,128)S(1)} %reduce.1) | data formatting | bytes 2097152
  313.6 9.7 %copy.42 = f32[8,1,8,4096]{3,2,0,1:T(8,128)S(1)} copy(f32[8,1,8,4096]{0,3,2,1:T(8,128)} %bitcast.61) | data formatting | bytes 2097152 | tf_op jit(solution)/shard_map/all_to_all | solution.py:48
  323.4 1.3 fusion.7
  324.7 1.6 convolution_subtract_fusion.1
  326.3 0.0 copy-start.4
  326.4 9.7 %fusion.6 = f32[64,256]{1,0:T(8,128)} fusion(f32[64,4096]{1,0:T(8,128)S(1)} %convolution_subtract_fusion.1, f32[256,4096]{1,0:T(8,128)} %bitcast.57, f32[256,1,4096]{2,1,0:T(1,128)} %param.11), kind=kOutput, calls=%fused_computation.18 | convolution fusion | flops 806354944 | bytes 9502720 | tf_op jit(solution)/shard_map/dot_general | solution.py:16
  336.0 0.0 all-reduce.7.cloned.1.call-update
  336.0 126.2 %all-reduce.7.cloned.1.call-done = (f32[64,256]{1,0:T(8,128)}, f32[256,256]{1,0:T(8,128)}) async-done(((f32[64,256]{1,0:T(8,128)}, f32[256,256]{1,0:T(8,128)}), (f32[64,256]{1,0:T(8,128)}, f32[256,256]{1,0:T(8,128)})) %all-reduce.7.cloned.1.call-update) | async-done | bytes 327696 | tf_op jit(solution)/shard_map/psum | solution.py:69
  462.3 1.8 multiply_reduce_fusion.2
  464.1 1.8 fusion.12
  467.2 0.0 copy-start.2
  467.2 3.5 fusion.28
  470.8 0.4 fusion.27
  471.2 15.2 %multiply_reduce_fusion = (f32[]{:T(128)}, f32[256,4096]{1,0:T(8,128)S(1)}) fusion(f32[256,4096]{1,0:T(8,128)} %bitcast.58, f32[256,4096]{1,0:T(8,128)S(1)} %fusion.28, f32[256,256]{1,0:T(8,128)S(1)} %fusion.27, f32[256,1,4096]{2,1,0:T(1,128)S(1)} %copy-done), kind=kOutput, calls=%fused_computation.11 | convolution fusion | flops 3226468352 | bytes 17039364 | tf_op jit(solution)/shard_map/dot_general | solution.py:16
  486.4 2.0 copy-done.1
  488.5 5.1 fusion.4
  493.5 41.6 %all-reduce.2 = (f32[]{:T(128)}, f32[]{:T(128)}) all-reduce(f32[]{:T(128)} %get-tuple-element.25, f32[]{:T(128)} %fusion.4), channel_id=1, replica_groups=mesh['frames'=8,'planes'=4] {'frames','planes'}, use_global_device_ids=true, to_apply=%region_12.13 | all-reduce | flops 2 | bytes 16 | tf_op jit(solution)/shard_map/psum | solution.py:78
  536.4 8.9 %maximum_bitcast_fusion = f32[256,1,4096]{2,0,1:T(8,128)S(1)} fusion(f32[256,4096]{1,0:T(8,128)} %copy-done.1, f32[]{:T(128)S(6)} %div.32, f32[256,4096]{1,0:T(8,128)} %bitcast.59, f32[256,1,4096]{2,1,0:T(1,128)} %param.11), kind=kLoop, calls=%fused_computation.10 | loop fusion | flops 4194304 | bytes 16777220 | tf_op jit(solution)/shard_map/reshape | solution.py:86
  545.3 6.3 %copy.41 = f32[256,1,4096]{2,1,0:T(1,128)} copy(f32[256,1,4096]{2,0,1:T(8,128)S(1)} %maximum_bitcast_fusion) | data formatting | bytes 8388608
  (20 shorter events, 0.1 us)
Async XLA Ops:
  14.2 5.3 copy-start.3
  208.9 16.8 %copy-start.5 = (s32[256,48]{0,1:T(8,128)S(1)}, s32[256,48]{0,1:T(8,128)}, u32[]{:S(2)}) copy-start(s32[256,48]{0,1:T(8,128)} %param.9) | copy-start | bytes 147460
  221.9 48.9 %all-to-all-start = ((f32[8,1,32768]{2,1,0:T(1,128)}), f32[8,1,32768]{2,1,0:T(1,128)S(1)}, u32[]{:S(2)}, u32[]{:S(2)}) async-start(f32[8,1,32768]{2,1,0:T(1,128)} %reshape.148), calls=%async_computation | async-start | bytes 2097152 | tf_op jit(solution)/shard_map/all_to_all | solution.py:48
  225.6 236.7 %all-reduce.7.cloned.1.call-start = ((), (), s32[]{:S(2)}) async-start(), calls=%async_computation.1 | async-start | bytes 655360 | tf_op jit(solution)/shard_map/psum | solution.py:69
  326.3 135.9 %copy-start.4 = (f32[64,256]{1,0:T(8,128)S(1)}, f32[64,256]{1,0:T(8,128)}, u32[]{:S(2)}) copy-start(f32[64,256]{1,0:T(8,128)} %param.10) | copy-start | bytes 196612
  467.2 4.0 copy-start
  467.2 19.2 %copy-start.2 = (f32[64,256]{1,0:T(8,128)}, f32[64,256]{1,0:T(8,128)S(1)}, u32[]{:S(2)}) copy-start(f32[64,256]{1,0:T(8,128)S(1)} %subtract_maximum_fusion) | copy-start | bytes 196612
  486.4 2.0 copy-start.1
Sparse Core Ops, SparseCore 0:
  336.2 126.0 all-reduce.6
where the time goes:
time: 566 us; the launch traced here: 559 us
  other arithmetic  178 us (31%)
  waiting for transfers between devices  126 us (22%)
  local copies, waits for them, and re-layouts  125 us (22%)
  blocking collectives  56 us (10%)
  matrix products  52.6 us (9%)
  between operations  17.2 us (3%)
    unnamed x1, other arithmetic  147 us
    psum x1, waiting for transfers between devices, body(): lax.psum((matmul(spatial, spatial.T), matmul(detrended, spatial.T)), ('fr...  126 us
    unnamed x20, local copies, waits for them, and re-layouts  71.8 us
    dot_general x10, matrix products, matmul(): jnp.dot(left_side, right_side, precision=lax.Precision.HIGHEST, preferred...  52.6 us
    psum x1, blocking collectives, body(): lax.psum((jnp.sum(spatial_grad * spatial_grad), jnp.sum(spatial_grad * ma...  41.6 us
    mul x1, local copies, waits for them, and re-layouts, body(): payload = flattened * weight[:, None, None]  23.8 us
    psum x1, blocking collectives, body(): lax.psum((numerator, energy, template_energy), 'planes')  14.3 us
    mul x1, other arithmetic, body(): spatial_init.reshape(components, plane_local * pixels_local) * support_mask  13.6 us
  transfers between devices with their start and end apart: 2, of which 1 were waited for; matrix products, arithmetic and copies ran while one was open for 8% of the time, Pallas kernels for 0%

commit v1 on v0

v1 whole, which is shorter than its diff:
```python
import functools

import jax
import jax.numpy as jnp
import numpy as np
from jax import lax
from jax.experimental import pallas as pl
from jax.experimental.pallas import tpu as pltpu
from jax.sharding import PartitionSpec as P

TILE = 1024
NTREND = 16
LANES = 128
SUBS = 8
MESH = pl.DeviceIdType.MESH
F32 = jnp.float32
BF16 = jnp.bfloat16
HIGH = lax.Precision.HIGH
HIGHEST = lax.Precision.HIGHEST

epsilon = 1e-06

NN = (((1,), (0,)), ((), ()))
NT = (((1,), (1,)), ((), ()))


def trend_projection(frame_count, basis_order):
    times = np.arange(frame_count) + 0.5
    orders = np.arange(basis_order)
    scales = np.where(orders == 0, np.sqrt(1.0 / frame_count), np.sqrt(2.0 / frame_count))
    basis = np.cos(np.pi * times[:, None] * orders[None, :] / frame_count) * scales[None, :]
    return (np.eye(frame_count) - basis @ basis.T).astype(np.float32)


def split(x):
    high = x.astype(BF16)
    return high, (x - high.astype(F32)).astype(BF16)


def dot1(a, b, dims=NN):
    return lax.dot_general(a, b, dims, preferred_element_type=F32)


def dot3(a, b, dims=NN):
    return dot1(a[0], b[0], dims) + (dot1(a[0], b[1], dims) + dot1(a[1], b[0], dims))


def fold(x):
    rows, columns = x.shape
    line = x[:, :LANES]
    for j in range(1, columns // LANES):
        line = line + x[:, j * LANES : (j + 1) * LANES]
    return jnp.sum(line.reshape(rows // SUBS, SUBS, LANES), axis=0)


def total(x):
    return jnp.sum(jnp.sum(x, axis=0, keepdims=True), axis=1, keepdims=True)


def register_kernel(shifts_ref, rec_ref, tmpl_ref, payload_ref, stats_ref, reg_ref):
    frames, height, width = rec_ref.shape
    tmpl = tmpl_ref[...]
    for f in range(frames):
        x = rec_ref[f]
        across = lax.rem(shifts_ref[f, 1] + width, width)
        down = lax.rem(shifts_ref[f, 0] + height, height)
        y = pltpu.roll(pltpu.roll(x, across, 1), down, 0)
        reg_ref[f * height : (f + 1) * height, :] = y
        stats_ref[f : f + 1, :] = jnp.sum(y * tmpl, axis=0, keepdims=True)
        stats_ref[frames + f : frames + f + 1, :] = jnp.sum(x * x, axis=0, keepdims=True)
    stats_ref[2 * frames :, :] = fold(tmpl * tmpl)
    for r in range(height):
        payload_ref[:, r * width : (r + 1) * width] = reg_ref[pl.ds(r, frames, stride=height), :]


def main_kernel(
    nf, nz, pixel_count,
    payload_ref, stats_ref, support_ref, proj_ref, w0_ref, h0_ref,
    temporal_ref, scal_ref, g_out, hm_out,
    hf, hhi, hlo, gbuf, rbuf, dbuf, cov, gram, gramx, wcol, zbuf,
    stz, stf, tgl, rs, tz, tgf, qz, qf, gz, gf, sems, lsem,
):
    f = lax.axis_index("frames")
    z = lax.axis_index("planes")
    comps, pixels = hf.shape
    total_frames = w0_ref.shape[0]
    fl = total_frames // nf
    tiles = pixels // TILE
    own = pl.ds(pl.multiple_of(f * fl, fl), fl)

    def over_frames(k, source, target):
        copies = []
        for d in range(1, nf):
            peer = lax.rem(f + d, nf)
            copies.append(
                pltpu.make_async_remote_copy(
                    src_ref=source(peer), dst_ref=target,
                    send_sem=sems.at[k, 0, d], recv_sem=sems.at[k, 1, d],
                    device_id=(peer, z), device_id_type=MESH,
                )
            )
        for copy in copies:
            copy.start()
        return copies

    def over_planes(k, source, target):
        copies = []
        for d in range(1, nz):
            peer = lax.rem(z + d, nz)
            copies.append(
                pltpu.make_async_remote_copy(
                    src_ref=source, dst_ref=target,
                    send_sem=sems.at[k, 0, d], recv_sem=sems.at[k, 1, d],
                    device_id=(f, peer), device_id_type=MESH,
                )
            )
        for copy in copies:
            copy.start()
        return copies

    def wait(copies):
        for copy in copies:
            copy.wait()

    load_h = pltpu.make_async_copy(h0_ref, hf, lsem.at[0])
    load_h.start()
    mine = pltpu.make_async_copy(
        payload_ref.at[:, pl.ds(pl.multiple_of(f * pixels, pixels), pixels)],
        rbuf.at[own, :], lsem.at[1],
    )
    mine.start()

    barrier = pltpu.get_barrier_semaphore()
    for d in range(1, nf):
        pl.semaphore_signal(barrier, inc=1, device_id=(lax.rem(f + d, nf), z), device_id_type=MESH)
    for d in range(1, nz):
        pl.semaphore_signal(barrier, inc=1, device_id=(f, lax.rem(z + d, nz)), device_id_type=MESH)
    pl.semaphore_wait(barrier, nf - 1 + nz - 1)

    stz[z] = stats_ref[...]
    plane_stats = over_planes(0, stats_ref, stz.at[z])
    pixel_copies = over_frames(
        1,
        lambda peer: payload_ref.at[:, pl.ds(pl.multiple_of(peer * pixels, pixels), pixels)],
        rbuf.at[own, :],
    )

    wait(plane_stats)
    summed = stz[0]
    for i in range(1, nz):
        summed = summed + stz[i]
    stf[f] = summed
    frame_stats = over_frames(2, lambda peer: stf.at[f], stf.at[f])

    load_h.wait()
    gram[...] = jnp.zeros_like(gram)
    gramx[...] = jnp.zeros_like(gramx)
    first_tile = z * (pixel_count // TILE) + f * tiles

    def prepare(c, carry):
        columns = pl.ds(pl.multiple_of(c * TILE, TILE), TILE)
        hit = jnp.where(support_ref[...] == first_tile + c, 1.0, 0.0).astype(F32)
        covered = jnp.broadcast_to(jnp.max(hit, axis=1, keepdims=True), (comps, LANES))
        cov[c] = covered
        h = hf[:, columns] * jnp.concatenate([covered] * (TILE // LANES), axis=1)
        hf[:, columns] = h
        high, low = split(h)
        hhi[:, columns] = high
        hlo[:, columns] = low
        gram[...] += dot1(high, high, NT)
        gramx[...] += dot1(high, low, NT)
        return carry

    lax.fori_loop(0, tiles, prepare, 0)
    save_h = pltpu.make_async_copy(hf, hm_out, lsem.at[2])
    save_h.start()
    gram[...] += gramx[...] + gramx[...].T
    w0 = w0_ref[...]
    tgl[...] = jnp.dot(w0, gram[...], precision=HIGHEST, preferred_element_type=F32)

    wait(frame_stats)
    template_energy = total(summed[2 * fl :, :])
    for s in range(nf):
        sums = stf[s]
        numerator = jnp.sum(sums[:fl], axis=1, keepdims=True)
        energy = jnp.sum(sums[fl : 2 * fl], axis=1, keepdims=True)
        weight = numerator / jnp.sqrt(energy * template_energy + epsilon)
        wcol[s * fl : (s + 1) * fl, :] = jnp.broadcast_to(weight, (fl, LANES))

    mine.wait()
    wait(pixel_copies)
    zbuf[...] = jnp.zeros_like(zbuf)

    def correlate(c, carry):
        columns = pl.ds(pl.multiple_of(c * TILE, TILE), TILE)
        series = rbuf[:, columns] * jnp.concatenate([wcol[...]] * (TILE // LANES), axis=1)
        rbuf[:, columns] = series
        zbuf[...] += dot3(split(series), (hhi[:, columns], hlo[:, columns]), NT)
        return carry

    lax.fori_loop(0, tiles, correlate, 0)
    tgl[...] -= jnp.dot(proj_ref[...], zbuf[...], precision=HIGHEST, preferred_element_type=F32)

    rs[f] = tgl[own, :]
    scatter = over_frames(
        3, lambda peer: tgl.at[pl.ds(pl.multiple_of(peer * fl, fl), fl), :], rs.at[f]
    )

    def detrend(c, carry):
        columns = pl.ds(pl.multiple_of(c * TILE, TILE), TILE)
        dbuf[:, columns] = dot3(split(proj_ref[...]), split(rbuf[:, columns]))
        return carry

    lax.fori_loop(0, tiles, detrend, 0)
    wait(scatter)
    part = rs[0]
    for i in range(1, nf):
        part = part + rs[i]
    tz[z] = part
    wait(over_planes(4, tz.at[z], tz.at[z]))
    part = tz[0]
    for i in range(1, nz):
        part = part + tz[i]
    tgf[own, :] = part
    wait(over_frames(5, lambda peer: tgf.at[own, :], tgf.at[own, :]))

    def all_sum(k, value, planes_buf, frames_buf):
        planes_buf[z] = value
        wait(over_planes(k, planes_buf.at[z], planes_buf.at[z]))
        value = planes_buf[0]
        for i in range(1, nz):
            value = value + planes_buf[i]
        frames_buf[f] = value
        wait(over_frames(k + 1, lambda peer: frames_buf.at[f], frames_buf.at[f]))
        value = frames_buf[0]
        for i in range(1, nf):
            value = value + frames_buf[i]
        return value

    grad = tgf[...]
    curve = fold(grad * jnp.dot(grad, gram[...], precision=HIGHEST, preferred_element_type=F32))
    curve = total(all_sum(6, curve, qz, qf))
    step = total(fold(grad * grad)) / (curve + epsilon)
    w1 = jnp.maximum(w0 - step * grad, 0.0)
    temporal_ref[...] = w1
    w1s = split(w1)
    w1t = split(w1.T)

    def gradient(c, carry):
        squares, curves = carry
        columns = pl.ds(pl.multiple_of(c * TILE, TILE), TILE)
        error = dot3(w1s, (hhi[:, columns], hlo[:, columns])) - dbuf[:, columns]
        g = dot3(w1t, split(error)) * jnp.concatenate([cov[c]] * (TILE // LANES), axis=1)
        gbuf[:, columns] = g
        bent = dot3(w1s, split(g))
        return squares + fold(g * g), curves + fold(bent * bent)

    nothing = jnp.zeros((SUBS, LANES), F32)
    squares, curves = lax.fori_loop(0, tiles, gradient, (nothing, nothing))
    save_g = pltpu.make_async_copy(gbuf, g_out, lsem.at[3])
    save_g.start()
    sums = all_sum(8, jnp.concatenate([squares, curves], axis=0), gz, gf)
    step = total(sums[:SUBS]) / (total(sums[SUBS:]) + epsilon)
    scal_ref[...] = jnp.broadcast_to(step, (SUBS, LANES))
    save_h.wait()
    save_g.wait()


def body(nf, nz, recording, template, shifts, support, temporal_init, spatial_init):
    frames, planes, height, width = recording.shape
    comps = spatial_init.shape[0]
    pixels = spatial_init.shape[1] * spatial_init.shape[2]
    pixel_count = height * width
    total_frames = temporal_init.shape[0]
    tiles = pixels // TILE
    vmem = pl.BlockSpec(memory_space=pltpu.VMEM)
    hbm = pl.BlockSpec(memory_space=pl.ANY)
    payload, stats = pl.pallas_call(
        register_kernel,
        out_shape=(
            jax.ShapeDtypeStruct((frames, pixel_count), F32),
            jax.ShapeDtypeStruct((2 * frames + SUBS, LANES), F32),
        ),
        in_specs=[pl.BlockSpec(memory_space=pltpu.SMEM), vmem, vmem],
        out_specs=(vmem, vmem),
        scratch_shapes=[pltpu.VMEM((frames * height, width), F32)],
        name="register",
    )(
        shifts.reshape(frames, 2),
        recording.reshape(frames, height, width),
        template.reshape(height, width),
    )
    count = max(nf, nz)
    temporal, scal, grad, masked = pl.pallas_call(
        functools.partial(main_kernel, nf, nz, pixel_count),
        out_shape=(
            jax.ShapeDtypeStruct((total_frames, comps), F32),
            jax.ShapeDtypeStruct((SUBS, LANES), F32),
            jax.ShapeDtypeStruct((comps, pixels), F32),
            jax.ShapeDtypeStruct((comps, pixels), F32),
        ),
        in_specs=[hbm, vmem, vmem, vmem, vmem, hbm],
        out_specs=(vmem, vmem, hbm, hbm),
        scratch_shapes=[
            pltpu.VMEM((comps, pixels), F32),
            pltpu.VMEM((comps, pixels), BF16),
            pltpu.VMEM((comps, pixels), BF16),
            pltpu.VMEM((comps, pixels), F32),
            pltpu.VMEM((total_frames, pixels), F32),
            pltpu.VMEM((total_frames, pixels), F32),
            pltpu.VMEM((tiles, comps, LANES), F32),
            pltpu.VMEM((comps, comps), F32),
            pltpu.VMEM((comps, comps), F32),
            pltpu.VMEM((total_frames, LANES), F32),
            pltpu.VMEM((total_frames, comps), F32),
            pltpu.VMEM((nz, 2 * frames + SUBS, LANES), F32),
            pltpu.VMEM((nf, 2 * frames + SUBS, LANES), F32),
            pltpu.VMEM((total_frames, comps), F32),
            pltpu.VMEM((nf, frames, comps), F32),
            pltpu.VMEM((nz, frames, comps), F32),
            pltpu.VMEM((total_frames, comps), F32),
            pltpu.VMEM((nz, SUBS, LANES), F32),
            pltpu.VMEM((nf, SUBS, LANES), F32),
            pltpu.VMEM((nz, 2 * SUBS, LANES), F32),
            pltpu.VMEM((nf, 2 * SUBS, LANES), F32),
            pltpu.SemaphoreType.DMA((10, 2, count)),
            pltpu.SemaphoreType.DMA((4,)),
        ],
        compiler_params=pltpu.CompilerParams(
            collective_id=0, has_side_effects=True, vmem_limit_bytes=40 * 1024 * 1024
        ),
        name="factorize",
    )(
        payload,
        stats,
        support,
        jnp.asarray(trend_projection(total_frames, NTREND)),
        temporal_init,
        spatial_init.reshape(comps, pixels),
    )
    spatial = jnp.maximum(masked - scal[0, 0] * grad, 0.0)
    return temporal, spatial.reshape(spatial_init.shape)


def solution(mesh):
    placed = (
        P("frames", "planes", None, None),
        P("planes", None, None),
        P("frames", "planes", None),
        P(),
        P(),
        P(None, "planes", "frames"),
    )
    return jax.shard_map(
        functools.partial(body, mesh.shape["frames"], mesh.shape["planes"]),
        mesh=mesh,
        in_specs=placed,
        out_specs=(P(), P(None, "planes", "frames")),
        check_vma=False,
    )
```

time: 566 us -> 75.2 us (0.13); the launches traced: 559 us -> 75 us
  other arithmetic: 178 us -> 1.33 us
  waiting for transfers between devices: 126 us -> 0 us
  local copies, waits for them, and re-layouts: 125 us -> 15.8 us
  Pallas kernels: 0 us -> 57.2 us
  blocking collectives: 56 us -> 0 us
  matrix products: 52.6 us -> 0 us
  between operations: 17.2 us -> 0.7 us
    unnamed x1 -> x0, other arithmetic: 147 us -> none
    psum x1 -> x0, waiting for transfers between devices: 126 us -> none  [body(): lax.psum((matmul(spatial, spatial.T), matmul(detrended, spatial.T)), ('fr...]
    unnamed x20 -> x12, local copies, waits for them, and re-layouts: 71.8 us -> 13.9 us
    pallas_call x0 -> x2, Pallas kernels: none -> 57.2 us  [the longest x1 53.7 us: body(): pl.pallas_call(functools.partial(main_kernel, nf, nz, pixel_count), out_s...]
    psum x2 -> x0, blocking collectives: 56 us -> none  [the longest x1 41.6 us: body(): lax.psum((jnp.sum(spatial_grad * spatial_grad), jnp.sum(spatial_grad * ma...]
    dot_general x10 -> x0, matrix products: 52.6 us -> none  [matmul(): jnp.dot(left_side, right_side, precision=lax.Precision.HIGHEST, preferred...]
    mul x2 -> x0, local copies, waits for them, and re-layouts: 23.9 us -> none  [the longest x1 23.8 us: body(): payload = flattened * weight[:, None, None]]
    mul x3 -> x0, other arithmetic: 13.8 us -> none  [the longest x1 13.6 us: body(): spatial_init.reshape(components, plane_local * pixels_local) * support_mask]
  transfers between devices with their start and end apart: 2 -> 0, of which waited for: 1 -> 0; matrix products, arithmetic and copies ran while one was open for 8% -> 0% of each run, Pallas kernels for 0% -> 0%
where the time goes in v1:
time: 75.2 us; the launch traced here: 75 us
  Pallas kernels  57.2 us (76%)
  local copies, waits for them, and re-layouts  15.8 us (21%)
  other arithmetic  1.33 us (2%)
    pallas_call x1, Pallas kernels, body(): pl.pallas_call(functools.partial(main_kernel, nf, nz, pixel_count), out_s...  53.7 us
    unnamed x12, local copies, waits for them, and re-layouts  13.9 us
    pallas_call x1, Pallas kernels, body(): pl.pallas_call(register_kernel, out_shape=(jax.ShapeDtypeStruct((frames,...  3.53 us

profile of v1, /device:TPU:0, one launch (start us, length us, event | category | flops | bytes accessed | tf_op | source)
XLA Modules:
  0.0 75.0 jit_solution(4701965677173014695)
XLA Ops:
  0.6 1.3 %copy.9.shifts_ref = s32[8,2]{1,0:T(8,128)} copy(s32[8,2]{0,1:T(2,128)} %bitcast.12) | data formatting | bytes 128 | tf_op jit(solution)/shard_map/reshape | solution.py:289
  2.0 0.9 %copy.10.support_ref = s32[256,48]{1,0:T(8,128)S(1)} copy(s32[256,48]{0,1:T(8,128)} %param.10) | data formatting | bytes 98304 | tf_op args[3]
  2.9 3.5 %register.1 = (f32[8,32768]{1,0:T(8,128)}, f32[24,128]{1,0:T(8,128)}) custom-call(s32[8,2]{1,0:T(8,128)} %copy.9.shifts_ref, f32[8,256,128]{2,1,0:T(8,128)} %bitcast.10, f32[256,128]{1,0:T(8,128)} %bitcast.11), custom_call_target="tpu_custom_call" | custom-call | tf_op jit(solution)/shard_map/register/pallas_call | solution.py:278
  6.4 0.0 copy-start
  6.4 0.0 copy-start.1
  6.4 0.0 copy-start.2
  6.4 0.0 copy-start.3
  6.4 6.1 %copy.14 = f32[256,1,4096]{2,0,1:T(8,128)S(1)} copy(f32[256,1,4096]{2,1,0:T(1,128)} %param.12) | data formatting | bytes 8388608
  12.5 0.0 copy-done
  12.5 0.0 copy-done.1
  12.5 0.0 copy-done.2
  12.5 0.0 copy-done.3
  12.5 53.7 %factorize.1 = (f32[64,256]{1,0:T(8,128)S(1)}, f32[8,128]{1,0:T(8,128)S(1)}, f32[256,4096]{1,0:T(8,128)S(1)}, f32[256,4096]{1,0:T(8,128)S(1)}) custom-call(f32[8,32768]{1,0:T(8,128)S(1)} %copy-done, f32[24,128]{1,0:T(8,128)S(1)} %copy-done.3, s32[256,48]{1,0:T(8,128)S(1)} %copy.10.support_ref, f32[64,64]{1,0:T(8,128)S(1)} %copy-done.2, ...), custom_call_target="tpu_custom_call" | custom-call | tf_op jit(solution)/shard_map/factorize/pallas_call | solution.py:294
  66.2 0.5 slice.3
  66.7 1.3 %maximum_bitcast_fusion = f32[256,1,4096]{2,0,1:T(8,128)S(1)} fusion(f32[256,4096]{1,0:T(8,128)S(1)} %get-tuple-element.11, f32[256,4096]{1,0:T(8,128)S(1)} %get-tuple-element.13, f32[]{:T(128)} %bitcast.3), kind=kLoop, calls=%fused_computation.1 | loop fusion | flops 3145728 | bytes 12582916 | tf_op jit(solution)/shard_map/reshape | solution.py:342
  68.0 6.3 %copy.11 = f32[256,1,4096]{2,1,0:T(1,128)} copy(f32[256,1,4096]{2,0,1:T(8,128)S(1)} %maximum_bitcast_fusion) | data formatting | bytes 8388608
  74.4 0.6 copy.16
Async XLA Ops:
  6.4 6.1 %copy-start = (f32[8,32768]{1,0:T(8,128)S(1)}, f32[8,32768]{1,0:T(8,128)}, u32[]{:S(2)}) copy-start(f32[8,32768]{1,0:T(8,128)} %get-tuple-element.8.payload_ref) | copy-start | bytes 3145732
  6.4 6.1 %copy-start.1 = (f32[64,256]{1,0:T(8,128)S(1)}, f32[64,256]{1,0:T(8,128)}, u32[]{:S(2)}) copy-start(f32[64,256]{1,0:T(8,128)} %w0_ref.1) | copy-start | bytes 196612
  6.4 6.1 %copy-start.2 = (f32[64,64]{1,0:T(8,128)S(1)}, f32[64,64]{1,0:T(8,128)}, u32[]{:S(2)}) copy-start(f32[64,64]{1,0:T(8,128)} %constant.4.clone.proj_ref) | copy-start | bytes 49156
  6.4 6.1 %copy-start.3 = (f32[24,128]{1,0:T(8,128)S(1)}, f32[24,128]{1,0:T(8,128)}, u32[]{:S(2)}) copy-start(f32[24,128]{1,0:T(8,128)} %get-tuple-element.9.stats_ref) | copy-start | bytes 36868

commit v2 on v1

--- a/solution.py
+++ b/solution.py
@@ -12,6 +12,7 @@
 NTREND = 16
 LANES = 128
 SUBS = 8
+FINISH = 8
 MESH = pl.DeviceIdType.MESH
 F32 = jnp.float32
 BF16 = jnp.bfloat16
@@ -41,8 +42,27 @@
     return lax.dot_general(a, b, dims, preferred_element_type=F32)
 
 
-def dot3(a, b, dims=NN):
-    return dot1(a[0], b[0], dims) + (dot1(a[0], b[1], dims) + dot1(a[1], b[0], dims))
+def stack(a):
+    return jnp.concatenate(a, axis=0)
+
+
+def dot_rows(stacked, high, low, dims=NN):
+    rows = stacked.shape[0] // 2
+    first = dot1(stacked, high, dims)
+    first = first[:rows] + first[rows:]
+    if low is None:
+        return first
+    return first + dot1(stacked[:rows], low, dims)
+
+
+def deep_left(x):
+    high, low = split(x)
+    return jnp.concatenate([high, low, high], axis=1)
+
+
+def deep_right(x):
+    high, low = split(x)
+    return jnp.concatenate([high, high, low], axis=0)
 
 
 def fold(x):
@@ -62,8 +82,8 @@
     tmpl = tmpl_ref[...]
     for f in range(frames):
         x = rec_ref[f]
-        across = lax.rem(shifts_ref[f, 1] + width, width)
-        down = lax.rem(shifts_ref[f, 0] + height, height)
+        across = lax.rem(shifts_ref[1, f] + width, width)
+        down = lax.rem(shifts_ref[0, f] + height, height)
         y = pltpu.roll(pltpu.roll(x, across, 1), down, 0)
         reg_ref[f * height : (f + 1) * height, :] = y
         stats_ref[f : f + 1, :] = jnp.sum(y * tmpl, axis=0, keepdims=True)
@@ -76,8 +96,8 @@
 def main_kernel(
     nf, nz, pixel_count,
     payload_ref, stats_ref, support_ref, proj_ref, w0_ref, h0_ref,
-    temporal_ref, scal_ref, g_out, hm_out,
-    hf, hhi, hlo, gbuf, rbuf, dbuf, cov, gram, gramx, wcol, zbuf,
+    temporal_ref, scal_ref, gbuf, hf,
+    hraw, hhi, hlo, rbuf, dbuf, cov, gram, gramx, wcol, zbuf,
     stz, stf, tgl, rs, tz, tgf, qz, qf, gz, gf, sems, lsem,
 ):
     f = lax.axis_index("frames")
@@ -122,13 +142,19 @@
         for copy in copies:
             copy.wait()
 
-    load_h = pltpu.make_async_copy(h0_ref, hf, lsem.at[0])
+    load_h = pltpu.make_async_copy(h0_ref, hraw, lsem.at[0])
     load_h.start()
-    mine = pltpu.make_async_copy(
-        payload_ref.at[:, pl.ds(pl.multiple_of(f * pixels, pixels), pixels)],
-        rbuf.at[own, :], lsem.at[1],
-    )
-    mine.start()
+    def part_of(device, c):
+        return pl.ds(pl.multiple_of(device * pixels + c * TILE, TILE), TILE)
+
+    mine = []
+    for c in range(tiles):
+        columns = pl.ds(c * TILE, TILE)
+        copy = pltpu.make_async_copy(
+            payload_ref.at[:, part_of(f, c)], rbuf.at[own, columns], lsem.at[1 + c]
+        )
+        copy.start()
+        mine.append(copy)
 
     barrier = pltpu.get_barrier_semaphore()
     for d in range(1, nf):
@@ -139,18 +165,21 @@
 
     stz[z] = stats_ref[...]
     plane_stats = over_planes(0, stats_ref, stz.at[z])
-    pixel_copies = over_frames(
-        1,
-        lambda peer: payload_ref.at[:, pl.ds(pl.multiple_of(peer * pixels, pixels), pixels)],
-        rbuf.at[own, :],
-    )
+    pixel_copies = [
+        over_frames(
+            9 + c,
+            lambda peer, c=c: payload_ref.at[:, part_of(peer, c)],
+            rbuf.at[own, pl.ds(c * TILE, TILE)],
+        )
+        for c in range(tiles)
+    ]
 
     wait(plane_stats)
     summed = stz[0]
     for i in range(1, nz):
         summed = summed + stz[i]
     stf[f] = summed
-    frame_stats = over_frames(2, lambda peer: stf.at[f], stf.at[f])
+    frame_stats = over_frames(1, lambda peer: stf.at[f], stf.at[f])
 
     load_h.wait()
     gram[...] = jnp.zeros_like(gram)
@@ -158,22 +187,26 @@
     first_tile = z * (pixel_count // TILE) + f * tiles
 
     def prepare(c, carry):
+        hit = jnp.where(support_ref[...] == first_tile + c, 1.0, 0.0).astype(F32)
+        row = jnp.max(hit, axis=0, keepdims=True)
+        covered = jnp.broadcast_to(row, (LANES, comps)).T
+        cov[c] = covered
+        for j in range(TILE // LANES):
+            columns = pl.ds(pl.multiple_of(c * TILE + j * LANES, LANES), LANES)
+            lines = pl.ds(c * (TILE // LANES) + j, comps, stride=pixels // LANES)
+            h = hraw[lines, :] * covered
+            hf[:, columns] = h
+            high, low = split(h)
+            hhi[:, columns] = high
+            hlo[:, columns] = low
         columns = pl.ds(pl.multiple_of(c * TILE, TILE), TILE)
-        hit = jnp.where(support_ref[...] == first_tile + c, 1.0, 0.0).astype(F32)
-        covered = jnp.broadcast_to(jnp.max(hit, axis=1, keepdims=True), (comps, LANES))
-        cov[c] = covered
-        h = hf[:, columns] * jnp.concatenate([covered] * (TILE // LANES), axis=1)
-        hf[:, columns] = h
-        high, low = split(h)
-        hhi[:, columns] = high
-        hlo[:, columns] = low
-        gram[...] += dot1(high, high, NT)
-        gramx[...] += dot1(high, low, NT)
+        both = jnp.concatenate([hhi[:, columns], hlo[:, columns]], axis=0)
+        product = dot1(both, hhi[:, columns], NT)
+        gram[...] += product[:comps]
+        gramx[...] += product[comps:]
         return carry
 
     lax.fori_loop(0, tiles, prepare, 0)
-    save_h = pltpu.make_async_copy(hf, hm_out, lsem.at[2])
-    save_h.start()
     gram[...] += gramx[...] + gramx[...].T
     w0 = w0_ref[...]
     tgl[...] = jnp.dot(w0, gram[...], precision=HIGHEST, preferred_element_type=F32)
@@ -187,28 +220,27 @@
         weight = numerator / jnp.sqrt(energy * template_energy + epsilon)
         wcol[s * fl : (s + 1) * fl, :] = jnp.broadcast_to(weight, (fl, LANES))
 
-    mine.wait()
-    wait(pixel_copies)
     zbuf[...] = jnp.zeros_like(zbuf)
-
-    def correlate(c, carry):
-        columns = pl.ds(pl.multiple_of(c * TILE, TILE), TILE)
+    for c in range(tiles):
+        mine[c].wait()
+        wait(pixel_copies[c])
+        columns = pl.ds(c * TILE, TILE)
         series = rbuf[:, columns] * jnp.concatenate([wcol[...]] * (TILE // LANES), axis=1)
         rbuf[:, columns] = series
-        zbuf[...] += dot3(split(series), (hhi[:, columns], hlo[:, columns]), NT)
-        return carry
-
-    lax.fori_loop(0, tiles, correlate, 0)
+        zbuf[...] += dot_rows(stack(split(series)), hhi[:, columns], hlo[:, columns], NT)
+
     tgl[...] -= jnp.dot(proj_ref[...], zbuf[...], precision=HIGHEST, preferred_element_type=F32)
 
     rs[f] = tgl[own, :]
     scatter = over_frames(
-        3, lambda peer: tgl.at[pl.ds(pl.multiple_of(peer * fl, fl), fl), :], rs.at[f]
+        2, lambda peer: tgl.at[pl.ds(pl.multiple_of(peer * fl, fl), fl), :], rs.at[f]
     )
+
+    proj = deep_left(proj_ref[...])
 
     def detrend(c, carry):
         columns = pl.ds(pl.multiple_of(c * TILE, TILE), TILE)
-        dbuf[:, columns] = dot3(split(proj_ref[...]), split(rbuf[:, columns]))
+        dbuf[:, columns] = dot1(proj, deep_right(rbuf[:, columns]))
         return carry
 
     lax.fori_loop(0, tiles, detrend, 0)
@@ -217,12 +249,12 @@
     for i in range(1, nf):
         part = part + rs[i]
     tz[z] = part
-    wait(over_planes(4, tz.at[z], tz.at[z]))
+    wait(over_planes(3, tz.at[z], tz.at[z]))
     part = tz[0]
     for i in range(1, nz):
         part = part + tz[i]
     tgf[own, :] = part
-    wait(over_frames(5, lambda peer: tgf.at[own, :], tgf.at[own, :]))
+    wait(over_frames(4, lambda peer: tgf.at[own, :], tgf.at[own, :]))
 
     def all_sum(k, value, planes_buf, frames_buf):
         planes_buf[z] = value
@@ -231,7 +263,7 @@
         for i in range(1, nz):
             value = value + planes_buf[i]
         frames_buf[f] = value
-        wait(over_frames(k + 1, lambda peer: frames_buf.at[f], frames_buf.at[f]))
+        wait(over_frames(k + 2, lambda peer: frames_buf.at[f], frames_buf.at[f]))
         value = frames_buf[0]
         for i in range(1, nf):
             value = value + frames_buf[i]
@@ -239,31 +271,49 @@
 
     grad = tgf[...]
     curve = fold(grad * jnp.dot(grad, gram[...], precision=HIGHEST, preferred_element_type=F32))
-    curve = total(all_sum(6, curve, qz, qf))
+    curve = total(all_sum(5, curve, qz, qf))
     step = total(fold(grad * grad)) / (curve + epsilon)
     w1 = jnp.maximum(w0 - step * grad, 0.0)
     temporal_ref[...] = w1
-    w1s = split(w1)
-    w1t = split(w1.T)
+    w1s = stack(split(w1))
+    w1t = deep_left(w1.T)
 
     def gradient(c, carry):
         squares, curves = carry
         columns = pl.ds(pl.multiple_of(c * TILE, TILE), TILE)
-        error = dot3(w1s, (hhi[:, columns], hlo[:, columns])) - dbuf[:, columns]
-        g = dot3(w1t, split(error)) * jnp.concatenate([cov[c]] * (TILE // LANES), axis=1)
+        error = dot_rows(w1s, hhi[:, columns], hlo[:, columns]) - dbuf[:, columns]
+        g = dot1(w1t, deep_right(error)) * jnp.concatenate([cov[c]] * (TILE // LANES), axis=1)
         gbuf[:, columns] = g
-        bent = dot3(w1s, split(g))
+        bent = dot_rows(w1s, g.astype(BF16), None)
         return squares + fold(g * g), curves + fold(bent * bent)
 
     nothing = jnp.zeros((SUBS, LANES), F32)
     squares, curves = lax.fori_loop(0, tiles, gradient, (nothing, nothing))
-    save_g = pltpu.make_async_copy(gbuf, g_out, lsem.at[3])
-    save_g.start()
-    sums = all_sum(8, jnp.concatenate([squares, curves], axis=0), gz, gf)
+    sums = all_sum(6, jnp.concatenate([squares, curves], axis=0), gz, gf)
     step = total(sums[:SUBS]) / (total(sums[SUBS:]) + epsilon)
     scal_ref[...] = jnp.broadcast_to(step, (SUBS, LANES))
-    save_h.wait()
-    save_g.wait()
+
+
+def finish_kernel(temporal_ref, scal_ref, g_ref, h_ref, temporal_out, spatial_out, buf, sems):
+    comps, pixels = h_ref.shape
+    lines = pixels // LANES
+    rows = comps // FINISH
+    step = jnp.broadcast_to(scal_ref[0:1, :], (rows, LANES))
+    first = pltpu.make_async_copy(temporal_ref, temporal_out, sems.at[FINISH])
+    first.start()
+    copies = []
+    for b in range(FINISH):
+        for j in range(lines):
+            block = (slice(b * rows, (b + 1) * rows), slice(j * LANES, (j + 1) * LANES))
+            value = jnp.maximum(h_ref[block] - step * g_ref[block], 0.0)
+            buf[pl.ds(b * rows * lines + j, rows, stride=lines), :] = value
+        part = pl.ds(b * rows * lines, rows * lines)
+        copy = pltpu.make_async_copy(buf.at[part, :], spatial_out.at[part, :], sems.at[b])
+        copy.start()
+        copies.append(copy)
+    first.wait()
+    for copy in copies:
+        copy.wait()
 
 
 def body(nf, nz, recording, template, shifts, support, temporal_init, spatial_init):
@@ -286,7 +336,7 @@
         scratch_shapes=[pltpu.VMEM((frames * height, width), F32)],
         name="register",
     )(
-        shifts.reshape(frames, 2),
+        shifts.reshape(frames, 2).T,
         recording.reshape(frames, height, width),
         template.reshape(height, width),
     )
@@ -300,12 +350,11 @@
             jax.ShapeDtypeStruct((comps, pixels), F32),
         ),
         in_specs=[hbm, vmem, vmem, vmem, vmem, hbm],
-        out_specs=(vmem, vmem, hbm, hbm),
+        out_specs=(vmem, vmem, vmem, vmem),
         scratch_shapes=[
-            pltpu.VMEM((comps, pixels), F32),
+            pltpu.VMEM((comps * pixels // LANES, LANES), F32),
             pltpu.VMEM((comps, pixels), BF16),
             pltpu.VMEM((comps, pixels), BF16),
-            pltpu.VMEM((comps, pixels), F32),
             pltpu.VMEM((total_frames, pixels), F32),
             pltpu.VMEM((total_frames, pixels), F32),
             pltpu.VMEM((tiles, comps, LANES), F32),
@@ -323,8 +372,8 @@
             pltpu.VMEM((nf, SUBS, LANES), F32),
             pltpu.VMEM((nz, 2 * SUBS, LANES), F32),
             pltpu.VMEM((nf, 2 * SUBS, LANES), F32),
-            pltpu.SemaphoreType.DMA((10, 2, count)),
-            pltpu.SemaphoreType.DMA((4,)),
+            pltpu.SemaphoreType.DMA((9 + tiles, 2, count)),
+            pltpu.SemaphoreType.DMA((1 + tiles,)),
         ],
         compiler_params=pltpu.CompilerParams(
             collective_id=0, has_side_effects=True, vmem_limit_bytes=40 * 1024 * 1024
@@ -333,12 +382,26 @@
     )(
         payload,
         stats,
-        support,
+        support.T,
         jnp.asarray(trend_projection(total_frames, NTREND)),
         temporal_init,
-        spatial_init.reshape(comps, pixels),
+        spatial_init.reshape(comps * pixels // LANES, LANES),
     )
-    spatial = jnp.maximum(masked - scal[0, 0] * grad, 0.0)
+    temporal, spatial = pl.pallas_call(
+        finish_kernel,
+        out_shape=(
+            jax.ShapeDtypeStruct((total_frames, comps), F32),
+            jax.ShapeDtypeStruct((comps * pixels // LANES, LANES), F32),
+        ),
+        in_specs=[vmem, vmem, vmem, vmem],
+        out_specs=(hbm, hbm),
+        scratch_shapes=[
+            pltpu.VMEM((comps * pixels // LANES, LANES), F32),
+            pltpu.SemaphoreType.DMA((FINISH + 1,)),
+        ],
+        compiler_params=pltpu.CompilerParams(vmem_limit_bytes=16 * 1024 * 1024),
+        name="finish",
+    )(temporal, scal, grad, masked)
     return temporal, spatial.reshape(spatial_init.shape)
 
 

time: 75.2 us -> 67.8 us (0.902)
  local copies, waits for them, and re-layouts: 15.8 us -> 6.51 us
  Pallas kernels: 57.2 us -> 60.2 us
  other arithmetic: 1.33 us -> 0 us
    unnamed x12, local copies, waits for them, and re-layouts: 13.9 us -> 6.51 us
    pallas_call x0 -> x1, Pallas kernels: none -> 5.04 us  [body(): pl.pallas_call(finish_kernel, out_shape=(jax.ShapeDtypeStruct((total_fram...]
    pallas_call x1, Pallas kernels: 53.7 us -> 51.6 us  [body(): pl.pallas_call(functools.partial(main_kernel, nf, nz, pixel_count), out_s...]
    reshape x1 -> x0, local copies, waits for them, and re-layouts: 1.35 us -> none  [body(): shifts.reshape(frames, 2)]
    reshape x1 -> x0, other arithmetic: 1.33 us -> none  [body(): return (temporal, spatial.reshape(spatial_init.shape))]
where the time goes in v2:
time: 67.8 us; the launch traced here: 67.3 us
  Pallas kernels  60.2 us (89%)
  local copies, waits for them, and re-layouts  6.51 us (10%)
    pallas_call x1, Pallas kernels, body(): pl.pallas_call(functools.partial(main_kernel, nf, nz, pixel_count), out_s...  51.6 us
    unnamed x12, local copies, waits for them, and re-layouts  6.51 us
    pallas_call x1, Pallas kernels, body(): pl.pallas_call(finish_kernel, out_shape=(jax.ShapeDtypeStruct((total_fram...  5.04 us
    pallas_call x1, Pallas kernels, body(): pl.pallas_call(register_kernel, out_shape=(jax.ShapeDtypeStruct((frames,...  3.53 us

profile of v2, /device:TPU:0, one launch (start us, length us, event | category | flops | bytes accessed | tf_op | source)
XLA Modules:
  0.0 67.3 jit_solution(12206479548624245819)
XLA Ops:
  0.6 3.5 %register.1 = (f32[8,32768]{1,0:T(8,128)}, f32[24,128]{1,0:T(8,128)}) custom-call(s32[2,8]{1,0:T(2,128)} %bitcast.12, f32[8,256,128]{2,1,0:T(8,128)} %bitcast.10, f32[256,128]{1,0:T(8,128)} %bitcast.11), custom_call_target="tpu_custom_call" | custom-call | tf_op jit(solution)/shard_map/register/pallas_call | solution.py:328
  4.2 0.0 copy-start
  4.2 2.2 %copy-done = f32[256,1,4096]{2,1,0:T(1,128)S(1)} copy-done((f32[256,1,4096]{2,1,0:T(1,128)S(1)}, f32[256,1,4096]{2,1,0:T(1,128)}, u32[]{:S(2)}) %copy-start) | copy-done | bytes 4194328
  6.3 0.0 copy-start.1
  6.3 1.2 %copy-done.1 = f32[8,32768]{1,0:T(8,128)S(1)} copy-done((f32[8,32768]{1,0:T(8,128)S(1)}, f32[8,32768]{1,0:T(8,128)}, u32[]{:S(2)}) %copy-start.1) | copy-done | bytes 1048600
  7.6 0.0 copy-start.2
  7.6 0.8 %copy-done.2 = f32[64,256]{1,0:T(8,128)S(1)} copy-done((f32[64,256]{1,0:T(8,128)S(1)}, f32[64,256]{1,0:T(8,128)}, u32[]{:S(2)}) %copy-start.2) | copy-done | bytes 65560
  8.4 0.0 copy-start.3
  8.4 0.8 %copy-done.3 = s32[256,48]{0,1:T(8,128)S(1)} copy-done((s32[256,48]{0,1:T(8,128)S(1)}, s32[256,48]{0,1:T(8,128)}, u32[]{:S(2)}) %copy-start.3) | copy-done | bytes 49176
  9.2 0.0 copy-start.4
  9.2 0.8 %copy-done.4 = f32[64,64]{1,0:T(8,128)S(1)} copy-done((f32[64,64]{1,0:T(8,128)S(1)}, f32[64,64]{1,0:T(8,128)}, u32[]{:S(2)}) %copy-start.4) | copy-done | bytes 16408
  10.0 0.0 copy-start.5
  10.0 0.7 %copy-done.5 = f32[24,128]{1,0:T(8,128)S(1)} copy-done((f32[24,128]{1,0:T(8,128)S(1)}, f32[24,128]{1,0:T(8,128)}, u32[]{:S(2)}) %copy-start.5) | copy-done | bytes 12312
  10.7 51.6 %factorize.1 = (f32[64,256]{1,0:T(8,128)S(1)}, f32[8,128]{1,0:T(8,128)S(1)}, f32[256,4096]{1,0:T(8,128)S(1)}, f32[256,4096]{1,0:T(8,128)S(1)}) custom-call(f32[8,32768]{1,0:T(8,128)S(1)} %copy-done.1, f32[24,128]{1,0:T(8,128)S(1)} %copy-done.5, s32[48,256]{1,0:T(8,128)S(1)} %bitcast.9, f32[64,64]{1,0:T(8,128)S(1)} %copy-done.4, f32[64,256]{1,0:T(8,128)S(1)} %copy-done.2, ...), custom_call_target="tpu_custom_call" | custom-call | tf_op jit(solution)/shard_map/factorize/pallas_call | solution.py:344
  62.3 5.0 %finish.1 = (f32[64,256]{1,0:T(8,128)}, f32[8192,128]{1,0:T(8,128)}) custom-call(f32[64,256]{1,0:T(8,128)S(1)} %get-tuple-element.12.temporal_ref, f32[8,128]{1,0:T(8,128)S(1)} %get-tuple-element.13.scal_ref, f32[256,4096]{1,0:T(8,128)S(1)} %get-tuple-element.14.g_ref, f32[256,4096]{1,0:T(8,128)S(1)} %get-tuple-element.15.h_ref), custom_call_target="tpu_custom_call" | custom-call | tf_op jit(solution)/shard_map/finish/pallas_call | solution.py:390
Async XLA Ops:
  4.2 2.2 %copy-start = (f32[256,1,4096]{2,1,0:T(1,128)S(1)}, f32[256,1,4096]{2,1,0:T(1,128)}, u32[]{:S(2)}) copy-start(f32[256,1,4096]{2,1,0:T(1,128)} %param.12) | copy-start | bytes 12582916
  6.3 1.2 %copy-start.1 = (f32[8,32768]{1,0:T(8,128)S(1)}, f32[8,32768]{1,0:T(8,128)}, u32[]{:S(2)}) copy-start(f32[8,32768]{1,0:T(8,128)} %get-tuple-element.10.payload_ref) | copy-start | bytes 3145732
  7.6 0.8 %copy-start.2 = (f32[64,256]{1,0:T(8,128)S(1)}, f32[64,256]{1,0:T(8,128)}, u32[]{:S(2)}) copy-start(f32[64,256]{1,0:T(8,128)} %w0_ref.1) | copy-start | bytes 196612
  8.4 0.8 %copy-start.3 = (s32[256,48]{0,1:T(8,128)S(1)}, s32[256,48]{0,1:T(8,128)}, u32[]{:S(2)}) copy-start(s32[256,48]{0,1:T(8,128)} %param.10) | copy-start | bytes 147460
  9.2 0.8 %copy-start.4 = (f32[64,64]{1,0:T(8,128)S(1)}, f32[64,64]{1,0:T(8,128)}, u32[]{:S(2)}) copy-start(f32[64,64]{1,0:T(8,128)} %constant.2.clone.proj_ref) | copy-start | bytes 49156
  10.0 0.7 %copy-start.5 = (f32[24,128]{1,0:T(8,128)S(1)}, f32[24,128]{1,0:T(8,128)}, u32[]{:S(2)}) copy-start(f32[24,128]{1,0:T(8,128)} %get-tuple-element.11.stats_ref) | copy-start | bytes 36868

commit v3 on v2

--- a/solution.py
+++ b/solution.py
@@ -13,11 +13,10 @@
 LANES = 128
 SUBS = 8
 FINISH = 8
+VMEM_LIMIT = 60 * 1000 * 1000
 MESH = pl.DeviceIdType.MESH
 F32 = jnp.float32
 BF16 = jnp.bfloat16
-HIGH = lax.Precision.HIGH
-HIGHEST = lax.Precision.HIGHEST
 
 epsilon = 1e-06
 
@@ -77,7 +76,7 @@
     return jnp.sum(jnp.sum(x, axis=0, keepdims=True), axis=1, keepdims=True)
 
 
-def register_kernel(shifts_ref, rec_ref, tmpl_ref, payload_ref, stats_ref, reg_ref):
+def register(shifts_ref, rec_ref, tmpl_ref, payload_ref, stats_ref, reg_ref):
     frames, height, width = rec_ref.shape
     tmpl = tmpl_ref[...]
     for f in range(frames):
@@ -95,10 +94,11 @@
 
 def main_kernel(
     nf, nz, pixel_count,
-    payload_ref, stats_ref, support_ref, proj_ref, w0_ref, h0_ref,
-    temporal_ref, scal_ref, gbuf, hf,
-    hraw, hhi, hlo, rbuf, dbuf, cov, gram, gramx, wcol, zbuf,
-    stz, stf, tgl, rs, tz, tgf, qz, qf, gz, gf, sems, lsem,
+    shifts_ref, rec_hbm, tmpl_hbm, support_hbm, proj_hbm, w0_hbm, h0_ref,
+    temporal_ref, h_out,
+    rec_ref, tmpl_ref, support_ref, proj_ref, w0_ref, payload_ref, stats_ref, reg_ref,
+    hraw, hhi, hlo, hf, gbuf, rbuf, dbuf, cov, gram, gramx, wcol, zbuf,
+    stz, stf, tgl, rs, tz, tgf, qf, gz, gf, gzs, gfull, sems, asem, lsem,
 ):
     f = lax.axis_index("frames")
     z = lax.axis_index("planes")
@@ -108,7 +108,7 @@
     tiles = pixels // TILE
     own = pl.ds(pl.multiple_of(f * fl, fl), fl)
 
-    def over_frames(k, source, target):
+    def over_frames(k, source, target, sems=sems):
         copies = []
         for d in range(1, nf):
             peer = lax.rem(f + d, nf)
@@ -123,13 +123,13 @@
             copy.start()
         return copies
 
-    def over_planes(k, source, target):
+    def over_planes(k, source, target, sems=sems):
         copies = []
         for d in range(1, nz):
             peer = lax.rem(z + d, nz)
             copies.append(
                 pltpu.make_async_remote_copy(
-                    src_ref=source, dst_ref=target,
+                    src_ref=source(peer), dst_ref=target,
                     send_sem=sems.at[k, 0, d], recv_sem=sems.at[k, 1, d],
                     device_id=(f, peer), device_id_type=MESH,
                 )
@@ -142,38 +142,49 @@
         for copy in copies:
             copy.wait()
 
-    load_h = pltpu.make_async_copy(h0_ref, hraw, lsem.at[0])
-    load_h.start()
+    def load(source, target, k):
+        copy = pltpu.make_async_copy(source, target, lsem.at[k])
+        copy.start()
+        return copy
+
+    load_rec = load(rec_hbm, rec_ref, 1)
+    load_tmpl = load(tmpl_hbm, tmpl_ref, 2)
     def part_of(device, c):
         return pl.ds(pl.multiple_of(device * pixels + c * TILE, TILE), TILE)
 
-    mine = []
-    for c in range(tiles):
-        columns = pl.ds(c * TILE, TILE)
-        copy = pltpu.make_async_copy(
-            payload_ref.at[:, part_of(f, c)], rbuf.at[own, columns], lsem.at[1 + c]
-        )
-        copy.start()
-        mine.append(copy)
+    peers = [(a, 0) for a in range(1, nf)] + [(0, b) for b in range(1, nz)]
+
+    def peer_of(a, b):
+        return (lax.rem(f + a, nf), lax.rem(z + b, nz))
 
     barrier = pltpu.get_barrier_semaphore()
-    for d in range(1, nf):
-        pl.semaphore_signal(barrier, inc=1, device_id=(lax.rem(f + d, nf), z), device_id_type=MESH)
-    for d in range(1, nz):
-        pl.semaphore_signal(barrier, inc=1, device_id=(f, lax.rem(z + d, nz)), device_id_type=MESH)
-    pl.semaphore_wait(barrier, nf - 1 + nz - 1)
+    for a, b in peers:
+        pl.semaphore_signal(barrier, inc=1, device_id=peer_of(a, b), device_id_type=MESH)
+
+    load_rec.wait()
+    load_tmpl.wait()
+    load_h = load(h0_ref, hraw, 0)
+    loads = [
+        load(support_hbm, support_ref, 3),
+        load(w0_hbm, w0_ref, 4),
+        load(proj_hbm, proj_ref, 5),
+    ]
+    register(shifts_ref, rec_ref, tmpl_ref, payload_ref, stats_ref, reg_ref)
+    pl.semaphore_wait(barrier, len(peers))
 
     stz[z] = stats_ref[...]
-    plane_stats = over_planes(0, stats_ref, stz.at[z])
+    plane_stats = over_planes(0, lambda peer: stats_ref, stz.at[z])
     pixel_copies = [
         over_frames(
-            9 + c,
+            8 + c,
             lambda peer, c=c: payload_ref.at[:, part_of(peer, c)],
             rbuf.at[own, pl.ds(c * TILE, TILE)],
         )
         for c in range(tiles)
     ]
 
+    for c in range(tiles):
+        rbuf[own, c * TILE : (c + 1) * TILE] = payload_ref[:, part_of(f, c)]
     wait(plane_stats)
     summed = stz[0]
     for i in range(1, nz):
@@ -182,6 +193,8 @@
     frame_stats = over_frames(1, lambda peer: stf.at[f], stf.at[f])
 
     load_h.wait()
+    for copy in loads:
+        copy.wait()
     gram[...] = jnp.zeros_like(gram)
     gramx[...] = jnp.zeros_like(gramx)
     first_tile = z * (pixel_count // TILE) + f * tiles
@@ -208,8 +221,14 @@
 
     lax.fori_loop(0, tiles, prepare, 0)
     gram[...] += gramx[...] + gramx[...].T
+    block = comps // nz
+    owned = pl.ds(pl.multiple_of(z * block, block), block)
+    gram_scatter = over_planes(
+        3, lambda peer: gram.at[pl.ds(pl.multiple_of(peer * block, block), block), :], gzs.at[z]
+    )
+    gzs[z] = gram[owned, :]
     w0 = w0_ref[...]
-    tgl[...] = jnp.dot(w0, gram[...], precision=HIGHEST, preferred_element_type=F32)
+    tgl[...] = dot_rows(stack(split(w0)), *split(gram[...]))
 
     wait(frame_stats)
     template_energy = total(summed[2 * fl :, :])
@@ -222,21 +241,26 @@
 
     zbuf[...] = jnp.zeros_like(zbuf)
     for c in range(tiles):
-        mine[c].wait()
+        if c == tiles - 1:
+            wait(gram_scatter)
+            part = gzs[0]
+            for i in range(1, nz):
+                part = part + gzs[i]
+            gfull[owned, :] = part
+            gram_gather = over_planes(4, lambda peer: gfull.at[owned, :], gfull.at[owned, :])
         wait(pixel_copies[c])
         columns = pl.ds(c * TILE, TILE)
         series = rbuf[:, columns] * jnp.concatenate([wcol[...]] * (TILE // LANES), axis=1)
         rbuf[:, columns] = series
         zbuf[...] += dot_rows(stack(split(series)), hhi[:, columns], hlo[:, columns], NT)
 
-    tgl[...] -= jnp.dot(proj_ref[...], zbuf[...], precision=HIGHEST, preferred_element_type=F32)
+    proj = deep_left(proj_ref[...])
+    tgl[...] -= dot1(proj, deep_right(zbuf[...]))
 
     rs[f] = tgl[own, :]
     scatter = over_frames(
         2, lambda peer: tgl.at[pl.ds(pl.multiple_of(peer * fl, fl), fl), :], rs.at[f]
     )
-
-    proj = deep_left(proj_ref[...])
 
     def detrend(c, carry):
         columns = pl.ds(pl.multiple_of(c * TILE, TILE), TILE)
@@ -249,29 +273,22 @@
     for i in range(1, nf):
         part = part + rs[i]
     tz[z] = part
-    wait(over_planes(3, tz.at[z], tz.at[z]))
+    wait(over_planes(5, lambda peer: tz.at[z], tz.at[z]))
     part = tz[0]
     for i in range(1, nz):
         part = part + tz[i]
     tgf[own, :] = part
-    wait(over_frames(4, lambda peer: tgf.at[own, :], tgf.at[own, :]))
-
-    def all_sum(k, value, planes_buf, frames_buf):
-        planes_buf[z] = value
-        wait(over_planes(k, planes_buf.at[z], planes_buf.at[z]))
-        value = planes_buf[0]
-        for i in range(1, nz):
-            value = value + planes_buf[i]
-        frames_buf[f] = value
-        wait(over_frames(k + 2, lambda peer: frames_buf.at[f], frames_buf.at[f]))
-        value = frames_buf[0]
-        for i in range(1, nf):
-            value = value + frames_buf[i]
-        return value
+    wait(over_frames(6, lambda peer: tgf.at[own, :], tgf.at[own, :]))
 
     grad = tgf[...]
-    curve = fold(grad * jnp.dot(grad, gram[...], precision=HIGHEST, preferred_element_type=F32))
-    curve = total(all_sum(5, curve, qz, qf))
+    wait(gram_gather)
+    bent = dot_rows(stack(split(grad)), *split(gfull[...]))
+    qf[f] = fold(grad * bent)
+    wait(over_frames(7, lambda peer: qf.at[f], qf.at[f]))
+    curve = qf[0]
+    for i in range(1, nf):
+        curve = curve + qf[i]
+    curve = total(curve)
     step = total(fold(grad * grad)) / (curve + epsilon)
     w1 = jnp.maximum(w0 - step * grad, 0.0)
     temporal_ref[...] = w1
@@ -289,29 +306,35 @@
 
     nothing = jnp.zeros((SUBS, LANES), F32)
     squares, curves = lax.fori_loop(0, tiles, gradient, (nothing, nothing))
-    sums = all_sum(6, jnp.concatenate([squares, curves], axis=0), gz, gf)
+    gz[z] = jnp.concatenate([squares, curves], axis=0)
+    wait(over_planes(0, lambda peer: gz.at[z], gz.at[z], asem))
+    sums = gz[0]
+    for i in range(1, nz):
+        sums = sums + gz[i]
+    gf[f] = sums
+    wait(over_frames(1, lambda peer: gf.at[f], gf.at[f], asem))
+    sums = gf[0]
+    for i in range(1, nf):
+        sums = sums + gf[i]
     step = total(sums[:SUBS]) / (total(sums[SUBS:]) + epsilon)
-    scal_ref[...] = jnp.broadcast_to(step, (SUBS, LANES))
-
-
-def finish_kernel(temporal_ref, scal_ref, g_ref, h_ref, temporal_out, spatial_out, buf, sems):
+    rows = comps // FINISH
+    for b in range(FINISH):
+        block = slice(b * rows, (b + 1) * rows)
+        h_out[block, :] = jnp.maximum(hf[block, :] - step * gbuf[block, :], 0.0)
+
+
+def finish_kernel(temporal_ref, h_ref, temporal_out, spatial_out, sems):
     comps, pixels = h_ref.shape
     lines = pixels // LANES
-    rows = comps // FINISH
-    step = jnp.broadcast_to(scal_ref[0:1, :], (rows, LANES))
-    first = pltpu.make_async_copy(temporal_ref, temporal_out, sems.at[FINISH])
+    first = pltpu.make_async_copy(temporal_ref, temporal_out, sems.at[lines])
     first.start()
-    copies = []
-    for b in range(FINISH):
-        for j in range(lines):
-            block = (slice(b * rows, (b + 1) * rows), slice(j * LANES, (j + 1) * LANES))
-            value = jnp.maximum(h_ref[block] - step * g_ref[block], 0.0)
-            buf[pl.ds(b * rows * lines + j, rows, stride=lines), :] = value
-        part = pl.ds(b * rows * lines, rows * lines)
-        copy = pltpu.make_async_copy(buf.at[part, :], spatial_out.at[part, :], sems.at[b])
+    copies = [first]
+    for j in range(lines):
+        copy = pltpu.make_async_copy(
+            h_ref.at[:, pl.ds(j * LANES, LANES)], spatial_out.at[:, j, :], sems.at[j]
+        )
         copy.start()
         copies.append(copy)
-    first.wait()
     for copy in copies:
         copy.wait()
 
@@ -324,37 +347,31 @@
     total_frames = temporal_init.shape[0]
     tiles = pixels // TILE
     vmem = pl.BlockSpec(memory_space=pltpu.VMEM)
-    hbm = pl.BlockSpec(memory_space=pl.ANY)
-    payload, stats = pl.pallas_call(
-        register_kernel,
-        out_shape=(
-            jax.ShapeDtypeStruct((frames, pixel_count), F32),
-            jax.ShapeDtypeStruct((2 * frames + SUBS, LANES), F32),
-        ),
-        in_specs=[pl.BlockSpec(memory_space=pltpu.SMEM), vmem, vmem],
-        out_specs=(vmem, vmem),
-        scratch_shapes=[pltpu.VMEM((frames * height, width), F32)],
-        name="register",
-    )(
-        shifts.reshape(frames, 2).T,
-        recording.reshape(frames, height, width),
-        template.reshape(height, width),
-    )
+    hbm = pl.BlockSpec(memory_space=pltpu.HBM)
+    smem = pl.BlockSpec(memory_space=pltpu.SMEM)
     count = max(nf, nz)
-    temporal, scal, grad, masked = pl.pallas_call(
+    temporal, refined = pl.pallas_call(
         functools.partial(main_kernel, nf, nz, pixel_count),
         out_shape=(
             jax.ShapeDtypeStruct((total_frames, comps), F32),
-            jax.ShapeDtypeStruct((SUBS, LANES), F32),
-            jax.ShapeDtypeStruct((comps, pixels), F32),
             jax.ShapeDtypeStruct((comps, pixels), F32),
         ),
-        in_specs=[hbm, vmem, vmem, vmem, vmem, hbm],
-        out_specs=(vmem, vmem, vmem, vmem),
+        in_specs=[smem] + [hbm] * 6,
+        out_specs=(vmem, vmem),
         scratch_shapes=[
+            pltpu.VMEM((frames, height, width), F32),
+            pltpu.VMEM((height, width), F32),
+            pltpu.VMEM((support.shape[1], comps), jnp.int32),
+            pltpu.VMEM((total_frames, total_frames), F32),
+            pltpu.VMEM((total_frames, comps), F32),
+            pltpu.VMEM((frames, pixel_count), F32),
+            pltpu.VMEM((2 * frames + SUBS, LANES), F32),
+            pltpu.VMEM((frames * height, width), F32),
             pltpu.VMEM((comps * pixels // LANES, LANES), F32),
             pltpu.VMEM((comps, pixels), BF16),
             pltpu.VMEM((comps, pixels), BF16),
+            pltpu.VMEM((comps, pixels), F32),
+            pltpu.VMEM((comps, pixels), F32),
             pltpu.VMEM((total_frames, pixels), F32),
             pltpu.VMEM((total_frames, pixels), F32),
             pltpu.VMEM((tiles, comps, LANES), F32),
@@ -368,20 +385,23 @@
             pltpu.VMEM((nf, frames, comps), F32),
             pltpu.VMEM((nz, frames, comps), F32),
             pltpu.VMEM((total_frames, comps), F32),
-            pltpu.VMEM((nz, SUBS, LANES), F32),
             pltpu.VMEM((nf, SUBS, LANES), F32),
             pltpu.VMEM((nz, 2 * SUBS, LANES), F32),
             pltpu.VMEM((nf, 2 * SUBS, LANES), F32),
-            pltpu.SemaphoreType.DMA((9 + tiles, 2, count)),
-            pltpu.SemaphoreType.DMA((1 + tiles,)),
+            pltpu.VMEM((nz, comps // nz, comps), F32),
+            pltpu.VMEM((comps, comps), F32),
+            pltpu.SemaphoreType.DMA((8 + tiles, 2, count)),
+            pltpu.SemaphoreType.DMA((2, 2, count)),
+            pltpu.SemaphoreType.DMA((6,)),
         ],
         compiler_params=pltpu.CompilerParams(
-            collective_id=0, has_side_effects=True, vmem_limit_bytes=40 * 1024 * 1024
+            collective_id=0, has_side_effects=True, vmem_limit_bytes=VMEM_LIMIT
         ),
         name="factorize",
     )(
-        payload,
-        stats,
+        shifts.reshape(frames, 2).T,
+        recording.reshape(frames, height, width),
+        template.reshape(height, width),
         support.T,
         jnp.asarray(trend_projection(total_frames, NTREND)),
         temporal_init,
@@ -391,17 +411,14 @@
         finish_kernel,
         out_shape=(
             jax.ShapeDtypeStruct((total_frames, comps), F32),
-            jax.ShapeDtypeStruct((comps * pixels // LANES, LANES), F32),
+            jax.ShapeDtypeStruct((comps, pixels // LANES, LANES), F32),
         ),
-        in_specs=[vmem, vmem, vmem, vmem],
+        in_specs=[vmem, vmem],
         out_specs=(hbm, hbm),
-        scratch_shapes=[
-            pltpu.VMEM((comps * pixels // LANES, LANES), F32),
-            pltpu.SemaphoreType.DMA((FINISH + 1,)),
-        ],
-        compiler_params=pltpu.CompilerParams(vmem_limit_bytes=16 * 1024 * 1024),
+        scratch_shapes=[pltpu.SemaphoreType.DMA((pixels // LANES + 1,))],
+        compiler_params=pltpu.CompilerParams(vmem_limit_bytes=1024 * 1024),
         name="finish",
-    )(temporal, scal, grad, masked)
+    )(temporal, refined)
     return temporal, spatial.reshape(spatial_init.shape)
 
 

time: 67.8 us -> 59.1 us (0.87)
  Pallas kernels: 60.2 us -> 55.2 us
  local copies, waits for them, and re-layouts: 6.51 us -> 3.02 us
    pallas_call x1 -> x0, Pallas kernels: 3.53 us -> none  [body(): pl.pallas_call(register_kernel, out_shape=(jax.ShapeDtypeStruct((frames,...]
    unnamed x12 -> x4, local copies, waits for them, and re-layouts: 6.51 us -> 3.02 us
    pallas_call x1, Pallas kernels: 5.04 us -> 2.29 us  [body(): pl.pallas_call(finish_kernel, out_shape=(jax.ShapeDtypeStruct((total_fram...]
    pallas_call x1, Pallas kernels: 51.6 us -> 52.9 us  [body(): pl.pallas_call(functools.partial(main_kernel, nf, nz, pixel_count), out_s...]
where the time goes in v3:
time: 59.1 us; the launch traced here: 58.9 us
  Pallas kernels  55.2 us (93%)
  local copies, waits for them, and re-layouts  3.02 us (5%)
  between operations  0.65 us (1%)
    pallas_call x1, Pallas kernels, body(): pl.pallas_call(functools.partial(main_kernel, nf, nz, pixel_count), out_s...  52.9 us
    unnamed x4, local copies, waits for them, and re-layouts  3.02 us
    pallas_call x1, Pallas kernels, body(): pl.pallas_call(finish_kernel, out_shape=(jax.ShapeDtypeStruct((total_fram...  2.29 us

profile of v3, /device:TPU:0, one launch (start us, length us, event | category | flops | bytes accessed | tf_op | source)
XLA Modules:
  0.0 58.9 jit_solution(552040898059432407)
XLA Ops:
  0.6 52.9 %factorize.1 = (f32[64,256]{1,0:T(8,128)}, f32[256,4096]{1,0:T(8,128)}) custom-call(s32[2,8]{1,0:T(2,128)} %bitcast.12, f32[8,256,128]{2,1,0:T(8,128)} %bitcast.9, f32[256,128]{1,0:T(8,128)} %bitcast.10, s32[48,256]{1,0:T(8,128)} %bitcast.11, f32[64,64]{1,0:T(8,128)} %constant.2.clone.proj_hbm, f32[64,256]{1,0:T(8,128)} %w0_hbm.1, f32[8192,128]{1,0:T(8,128)} %bitcast.8), custom_call_target="tpu_custom_call" | custom-call | tf_op jit(solution)/shard_map/factorize/pallas_call | solution.py:353
  53.6 0.0 copy-start
  53.6 2.2 %copy-done = f32[256,4096]{1,0:T(8,128)S(1)} copy-done((f32[256,4096]{1,0:T(8,128)S(1)}, f32[256,4096]{1,0:T(8,128)}, u32[]{:S(2)}) %copy-start) | copy-done | bytes 4194328
  55.7 0.0 copy-start.1
  55.7 0.8 %copy-done.1 = f32[64,256]{1,0:T(8,128)S(1)} copy-done((f32[64,256]{1,0:T(8,128)S(1)}, f32[64,256]{1,0:T(8,128)}, u32[]{:S(2)}) %copy-start.1) | copy-done | bytes 65560
  56.6 2.3 %finish.1 = (f32[64,256]{1,0:T(8,128)}, f32[256,32,128]{2,1,0:T(8,128)}) custom-call(f32[64,256]{1,0:T(8,128)S(1)} %copy-done.1, f32[256,4096]{1,0:T(8,128)S(1)} %copy-done), custom_call_target="tpu_custom_call" | custom-call | tf_op jit(solution)/shard_map/finish/pallas_call | solution.py:410
Async XLA Ops:
  53.6 2.2 %copy-start = (f32[256,4096]{1,0:T(8,128)S(1)}, f32[256,4096]{1,0:T(8,128)}, u32[]{:S(2)}) copy-start(f32[256,4096]{1,0:T(8,128)} %get-tuple-element.7.h_ref) | copy-start | bytes 12582916
  55.7 0.8 %copy-start.1 = (f32[64,256]{1,0:T(8,128)S(1)}, f32[64,256]{1,0:T(8,128)}, u32[]{:S(2)}) copy-start(f32[64,256]{1,0:T(8,128)} %get-tuple-element.6.temporal_ref) | copy-start | bytes 196612

commit v4 on v3

--- a/solution.py
+++ b/solution.py
@@ -241,7 +241,7 @@
 
     zbuf[...] = jnp.zeros_like(zbuf)
     for c in range(tiles):
-        if c == tiles - 1:
+        if c == max(tiles - 2, 0):
             wait(gram_scatter)
             part = gzs[0]
             for i in range(1, nz):

time: 59.1 us -> 58.8 us (level)
  no operation moved by 1% of the time
where the time goes in v4:
time: 58.8 us; the launch traced here: 58.5 us
  Pallas kernels  54.9 us (93%)
  local copies, waits for them, and re-layouts  3.02 us (5%)
  between operations  0.65 us (1%)
    pallas_call x1, Pallas kernels, body(): pl.pallas_call(functools.partial(main_kernel, nf, nz, pixel_count), out_s...  52.6 us
    unnamed x4, local copies, waits for them, and re-layouts  3.02 us
    pallas_call x1, Pallas kernels, body(): pl.pallas_call(finish_kernel, out_shape=(jax.ShapeDtypeStruct((total_fram...  2.29 us

profile of v4, /device:TPU:0, one launch (start us, length us, event | category | flops | bytes accessed | tf_op | source)
XLA Modules:
  0.0 58.5 jit_solution(16570141439709640945)
XLA Ops:
  0.6 52.6 %factorize.1 = (f32[64,256]{1,0:T(8,128)}, f32[256,4096]{1,0:T(8,128)}) custom-call(s32[2,8]{1,0:T(2,128)} %bitcast.12, f32[8,256,128]{2,1,0:T(8,128)} %bitcast.9, f32[256,128]{1,0:T(8,128)} %bitcast.10, s32[48,256]{1,0:T(8,128)} %bitcast.11, f32[64,64]{1,0:T(8,128)} %constant.2.clone.proj_hbm, f32[64,256]{1,0:T(8,128)} %w0_hbm.1, f32[8192,128]{1,0:T(8,128)} %bitcast.8), custom_call_target="tpu_custom_call" | custom-call | tf_op jit(solution)/shard_map/factorize/pallas_call | solution.py:353
  53.2 0.0 copy-start
  53.2 2.2 %copy-done = f32[256,4096]{1,0:T(8,128)S(1)} copy-done((f32[256,4096]{1,0:T(8,128)S(1)}, f32[256,4096]{1,0:T(8,128)}, u32[]{:S(2)}) %copy-start) | copy-done | bytes 4194328
  55.4 0.0 copy-start.1
  55.4 0.8 %copy-done.1 = f32[64,256]{1,0:T(8,128)S(1)} copy-done((f32[64,256]{1,0:T(8,128)S(1)}, f32[64,256]{1,0:T(8,128)}, u32[]{:S(2)}) %copy-start.1) | copy-done | bytes 65560
  56.3 2.3 %finish.1 = (f32[64,256]{1,0:T(8,128)}, f32[256,32,128]{2,1,0:T(8,128)}) custom-call(f32[64,256]{1,0:T(8,128)S(1)} %copy-done.1, f32[256,4096]{1,0:T(8,128)S(1)} %copy-done), custom_call_target="tpu_custom_call" | custom-call | tf_op jit(solution)/shard_map/finish/pallas_call | solution.py:410
Async XLA Ops:
  53.2 2.2 %copy-start = (f32[256,4096]{1,0:T(8,128)S(1)}, f32[256,4096]{1,0:T(8,128)}, u32[]{:S(2)}) copy-start(f32[256,4096]{1,0:T(8,128)} %get-tuple-element.7.h_ref) | copy-start | bytes 12582916
  55.4 0.8 %copy-start.1 = (f32[64,256]{1,0:T(8,128)S(1)}, f32[64,256]{1,0:T(8,128)}, u32[]{:S(2)}) copy-start(f32[64,256]{1,0:T(8,128)} %get-tuple-element.6.temporal_ref) | copy-start | bytes 196612
